TPU v7x, 512 devices: a whole 4x8x8 slice. The times are simulated.
512 devices in a mesh: sen: 32 (over y, z_hi), par: 16 (over x, z_lo, core).
Axes of the slice: x: 4, y: 8, z: 8 (z_hi: 4, z_lo: 2; z = z_hi * 2 + z_lo), core: 2. Of those that a mesh axis runs over, the one named last changes fastest.
Arguments:
- vectors: float32 [2, 256, 256], P(None, 'sen'), may hold values from -6 to 6
- observed: float32 [2, 256, 256], P(None, 'sen'), may hold values from -6 to 6
- operator: bfloat16 [2, 128, 256, 6144], P(None, None, 'sen', 'par'), may hold values from -0.15625 to 0.15625
- noise: float32 [256], P('sen'), may hold values from 0.3 to 3
- coefficient: float32 [16, 384], P('par'), may hold values from 0.05 to 0.24
- offsets: int32 [16, 384], P('par'), may hold values from -3 to 3
Outputs:
- residual: float32 [2, 256, 256], P(None, 'sen')
- applied: float32 [2, 256, 256], P(None, 'sen')
All inputs are finite; a program needn't handle non-finite values.
Results may differ from a plain program's by a relative error of at most 0.0018.
Values may be sent and summed in bfloat16 or wider, within the bound.
A program may use at most 64 MiB of HBM per device.

v0:
```python
import math
import jax
import jax.numpy as jnp
from jax import lax
from jax.sharding import PartitionSpec as P

SWEEPS = 4


def padded_2(cells, sides, width):
    for axis, dim in sides:
        count = lax.axis_size(axis)
        ends = count - 1
        head = lax.slice_in_dim(cells, 0, width, axis=dim)
        tail = lax.slice_in_dim(cells, cells.shape[dim] - width, cells.shape[dim], axis=dim)
        cells = jnp.concatenate(
            [
                lax.ppermute(tail, axis, [(i, (i + 1) % count) for i in range(ends)]),
                cells,
                lax.ppermute(head, axis, [((i + 1) % count, i) for i in range(ends)]),
            ],
            axis=dim,
        )
    return cells


def make_basis(length):
    half = length // 2
    times = jnp.arange(length, dtype=jnp.int32)[:, None]
    freqs = jnp.arange(half, dtype=jnp.int32)[None, :]
    phase = (2 * freqs + 1) * times % (2 * length)
    angle = phase.astype(jnp.float32) * (math.pi / length)
    scale = math.sqrt(2.0 / length)
    return jnp.concatenate([jnp.cos(angle), jnp.sin(angle)], axis=1) * scale


def sweep_once(field, padded, coefficient, offsets):
    width = field.shape[-1]
    upper = padded[..., :-2, :]
    lower = padded[..., 2:, :]
    lower_pad = jnp.pad(lower, ((0, 0), (0, 0), (0, 0), (0, 0), (3, 3)))
    linked = jnp.zeros_like(field)
    for shift in range(-3, 4):
        linked = linked + jnp.where(
            offsets == shift, lower_pad[..., 3 + shift : 3 + shift + width], 0.0
        )
    sides = jnp.pad(field, ((0, 0), (0, 0), (0, 0), (0, 0), (1, 1)))
    return field + coefficient * (sides[..., :-2] + sides[..., 2:] + upper + linked - 4.0 * field)


def smooth(field, coefficient, offsets, extend):
    for sweep in range(SWEEPS):
        field = sweep_once(field, extend(field), coefficient, offsets)
    return field


def forward_part(operator, piece):
    count = piece.shape[1]
    rows = piece.shape[2]
    flat = piece.reshape(2, count, rows, piece.shape[3] * piece.shape[4])
    real = jnp.einsum(
        "fsp,frp->frs", operator[0], flat[0], preferred_element_type=jnp.float32
    ) - jnp.einsum("fsp,frp->frs", operator[1], flat[1], preferred_element_type=jnp.float32)
    imag = jnp.einsum(
        "fsp,frp->frs", operator[0], flat[1], preferred_element_type=jnp.float32
    ) + jnp.einsum("fsp,frp->frs", operator[1], flat[0], preferred_element_type=jnp.float32)
    return jnp.stack([real, imag])


def extend_whole(field):
    return padded_2(field, (("par", 3),), 1)


def hessian(record, operator, noise, coefficient, offsets, basis):
    rows, sensors, length = record.shape
    half = length // 2
    grid_rows, width = coefficient.shape
    spectrum = jnp.dot(
        record.reshape(rows * sensors, length), basis, precision=lax.Precision.HIGHEST
    )
    spectrum = spectrum.reshape(rows, sensors, 2, half).transpose(2, 3, 0, 1).astype(jnp.bfloat16)
    real = jnp.einsum(
        "frs,fsp->frp", spectrum[0], operator[0], preferred_element_type=jnp.float32
    ) + jnp.einsum("frs,fsp->frp", spectrum[1], operator[1], preferred_element_type=jnp.float32)
    imag = jnp.einsum(
        "frs,fsp->frp", spectrum[1], operator[0], preferred_element_type=jnp.float32
    ) - jnp.einsum("frs,fsp->frp", spectrum[0], operator[1], preferred_element_type=jnp.float32)
    partial_value = jnp.stack([real, imag]).reshape(2, half, rows, grid_rows, width)
    adjoint = lax.psum(partial_value, "sen")
    smoothed = smooth(adjoint, coefficient, offsets, extend_whole)
    prior = smoothed.astype(jnp.bfloat16)
    forward = forward_part(operator, prior)
    forward = lax.psum(forward, "par")
    forward = forward.transpose(2, 3, 0, 1).reshape(rows * sensors, length)
    back = jnp.dot(forward, basis.T, precision=lax.Precision.HIGHEST).reshape(rows, sensors, length)
    return back + noise[None, :, None] * record


def body(vectors, observed, operator, noise, coefficient, offsets):
    basis = make_basis(vectors.shape[-1])
    residual = observed - hessian(vectors, operator, noise, coefficient, offsets, basis)
    applied = hessian(residual, operator, noise, coefficient, offsets, basis)
    return (residual, applied)


def solution(mesh):
    placed = (
        P(None, "sen", None),
        P(None, "sen", None),
        P(None, None, "sen", "par"),
        P("sen"),
        P("par", None),
        P("par", None),
    )
    return jax.shard_map(
        body,
        mesh=mesh,
        in_specs=placed,
        out_specs=(P(None, "sen", None), P(None, "sen", None)),
        check_vma=False,
    )
```

profile of v0, /device:TPU:32, one launch (start us, length us, event | category | flops | bytes accessed | tf_op | source)
XLA Modules:
  0.0 1003.8 jit_solution(16166331370840971243)
XLA Ops:
  8.9 1.6 fusion.64
  13.1 324.0 %all-reduce.19.cloned.1.call-done = f32[2,128,2,1,384]{4,2,1,0,3:T(2,128)} async-done(((f32[2,128,2,1,384]{4,2,1,0,3:T(2,128)}), f32[2,128,2,1,384]{4,2,1,0,3:T(2,128)}) %all-reduce.19.cloned.1.call-update) | async-done | bytes 786448 | tf_op jit(solution)/shard_map/psum | solution.py:89
  337.1 1.3 collective-permute-start
  338.4 1.3 collective-permute-start.1
  340.5 3.3 collective-permute-done.1
  343.8 8.0 multiply_add_fusion.5
  351.8 18.0 %collective-permute-start.2 = (f32[2,128,2,1,384]{4,2,1,0,3:T(2,128)S(1)}, f32[2,128,2,1,384]{4,2,1,0,3:T(2,128)S(1)}, u32[]{:S(2)}, u32[]{:S(2)}) collective-permute-start(f32[2,128,2,1,384]{4,2,1,0,3:T(2,128)S(1)} %multiply_add_fusion.5), channel_id=1, source_target_pairs={{0,1},{1,2},{2,3},{3,4},{4,5},{5,6},{6,7},{7,8},{8,9},{9,10},{10,1... | collective-permute-start | bytes 2359304 | tf_op jit(solution)/shard_map/ppermute | solution.py:18
  371.6 2.3 collective-permute-done.3
  374.0 6.8 multiply_add_fusion.4
  380.8 16.4 %collective-permute-start.4 = (f32[2,128,2,1,384]{4,2,1,0,3:T(2,128)S(1)}, f32[2,128,2,1,384]{4,2,1,0,3:T(2,128)S(1)}, u32[]{:S(2)}, u32[]{:S(2)}) collective-permute-start(f32[2,128,2,1,384]{4,2,1,0,3:T(2,128)S(1)} %multiply_add_fusion.4), channel_id=1, source_target_pairs={{0,1},{1,2},{2,3},{3,4},{4,5},{5,6},{6,7},{7,8},{8,9},{9,10},{10,1... | collective-permute-start | bytes 2359304 | tf_op jit(solution)/shard_map/ppermute | solution.py:18
  399.0 2.3 collective-permute-done.5
  401.4 6.8 multiply_add_fusion.3
  408.2 17.8 %collective-permute-start.6 = (f32[2,128,2,1,384]{4,2,1,0,3:T(2,128)S(1)}, f32[2,128,2,1,384]{4,2,1,0,3:T(2,128)}, u32[]{:S(2)}, u32[]{:S(2)}) collective-permute-start(f32[2,128,2,1,384]{4,2,1,0,3:T(2,128)S(1)} %multiply_add_fusion.3), channel_id=1, source_target_pairs={{0,1},{1,2},{2,3},{3,4},{4,5},{5,6},{6,7},{7,8},{8,9},{9,10},{10,1... | collective-permute-start | bytes 2359304 | tf_op jit(solution)/shard_map/ppermute | solution.py:18
  426.0 1.5 collective-permute-start.7
  427.7 2.7 collective-permute-done.7
  430.3 9.9 add_convert_fusion.1
  442.4 66.4 %psum.29 = f32[2,8,256]{2,1,0:T(8,128)S(1)} all-reduce(f32[2,8,256]{2,1,0:T(8,128)S(1)} %copy_bitcast_fusion.1), channel_id=1, replica_groups=mesh['sen'=32,'par'=16] {'par'}, use_global_device_ids=true, to_apply=%region_1.2 | all-reduce | flops 4096 | bytes 32768 | tf_op jit(solution)/shard_map/psum | solution.py:93
  512.7 314.5 %all-reduce.21.cloned.1.call-done = f32[2,128,2,1,384]{4,2,1,0,3:T(2,128)} async-done(((f32[2,128,2,1,384]{4,2,1,0,3:T(2,128)}), f32[2,128,2,1,384]{4,2,1,0,3:T(2,128)}) %all-reduce.21.cloned.1.call-update) | async-done | bytes 786448 | tf_op jit(solution)/shard_map/psum | solution.py:89
  827.2 1.3 collective-permute-start.8
  830.6 3.3 collective-permute-done.9
  833.9 8.0 multiply_add_fusion.2
  841.9 18.0 %collective-permute-start.10 = (f32[2,128,2,1,384]{4,2,1,0,3:T(2,128)S(1)}, f32[2,128,2,1,384]{4,2,1,0,3:T(2,128)S(1)}, u32[]{:S(2)}, u32[]{:S(2)}) collective-permute-start(f32[2,128,2,1,384]{4,2,1,0,3:T(2,128)S(1)} %multiply_add_fusion.2), channel_id=1, source_target_pairs={{0,1},{1,2},{2,3},{3,4},{4,5},{5,6},{6,7},{7,8},{8,9},{9,10},{10,1... | collective-permute-start | bytes 2359304 | tf_op jit(solution)/shard_map/ppermute | solution.py:18
  859.9 1.5 collective-permute-start.11
  861.8 2.3 collective-permute-done.11
  864.1 6.8 multiply_add_fusion.1
  870.9 16.4 %collective-permute-start.12 = (f32[2,128,2,1,384]{4,2,1,0,3:T(2,128)S(1)}, f32[2,128,2,1,384]{4,2,1,0,3:T(2,128)S(1)}, u32[]{:S(2)}, u32[]{:S(2)}) collective-permute-start(f32[2,128,2,1,384]{4,2,1,0,3:T(2,128)S(1)} %multiply_add_fusion.1), channel_id=1, source_target_pairs={{0,1},{1,2},{2,3},{3,4},{4,5},{5,6},{6,7},{7,8},{8,9},{9,10},{10,1... | collective-permute-start | bytes 2359304 | tf_op jit(solution)/shard_map/ppermute | solution.py:18
  889.2 2.3 collective-permute-done.13
  891.5 6.8 multiply_add_fusion
  898.3 17.0 %collective-permute-start.14 = (f32[2,128,2,1,384]{4,2,1,0,3:T(2,128)S(1)}, f32[2,128,2,1,384]{4,2,1,0,3:T(2,128)S(1)}, u32[]{:S(2)}, u32[]{:S(2)}) collective-permute-start(f32[2,128,2,1,384]{4,2,1,0,3:T(2,128)S(1)} %multiply_add_fusion), channel_id=1, source_target_pairs={{0,1},{1,2},{2,3},{3,4},{4,5},{5,6},{6,7},{7,8},{8,9},{9,10},{10,1... | collective-permute-start | bytes 2359304 | tf_op jit(solution)/shard_map/ppermute | solution.py:18
  917.2 2.3 collective-permute-done.15
  919.5 6.8 add_convert_fusion
  928.5 67.5 %psum.31 = f32[2,8,256]{2,1,0:T(8,128)S(1)} all-reduce(f32[2,8,256]{2,1,0:T(8,128)S(1)} %copy_bitcast_fusion), channel_id=1, replica_groups=mesh['sen'=32,'par'=16] {'par'}, use_global_device_ids=true, to_apply=%region_3.4 | all-reduce | flops 4096 | bytes 32768 | tf_op jit(solution)/shard_map/psum | solution.py:93
  (68 shorter events, 24.1 us)
Async XLA Ops:
  7.2 3.3 copy-start
  7.2 329.9 %all-reduce.19.cloned.1.call-start = ((), (), s32[]{:S(2)}) async-start(), calls=%async_computation | async-start | bytes 1572864 | tf_op jit(solution)/shard_map/psum | solution.py:89
  11.8 328.0 %copy-start.5 = (f32[1,384]{1,0:T(1,128)S(1)}, f32[1,384]{1,0:T(1,128)}, u32[]{:S(2)}) copy-start(f32[1,384]{1,0:T(1,128)} %param.10) | copy-start | bytes 4612
  11.8 328.0 %copy-start.6 = (s32[1,384]{1,0:T(1,128)S(1)}, s32[1,384]{1,0:T(1,128)}, u32[]{:S(2)}) copy-start(s32[1,384]{1,0:T(1,128)} %param.11) | copy-start | bytes 4612
  13.1 814.2 %all-reduce.21.cloned.1.call-start = ((), (), s32[]{:S(2)}) async-start(), calls=%async_computation.1 | async-start | bytes 1572864 | tf_op jit(solution)/shard_map/psum | solution.py:89
  337.1 3.4 collective-permute-start
  338.4 5.3 collective-permute-start.1
  351.8 19.8 %collective-permute-start.2 = (f32[2,128,2,1,384]{4,2,1,0,3:T(2,128)S(1)}, f32[2,128,2,1,384]{4,2,1,0,3:T(2,128)S(1)}, u32[]{:S(2)}, u32[]{:S(2)}) collective-permute-start(f32[2,128,2,1,384]{4,2,1,0,3:T(2,128)S(1)} %multiply_add_fusion.5), channel_id=1, source_target_pairs={{0,1},{1,2},{2,3},{3,4},{4,5},{5,6},{6,7},{7,8},{8,9},{9,10},{10,1... | collective-permute-start | bytes 2359304 | tf_op jit(solution)/shard_map/ppermute | solution.py:18
  369.8 4.2 collective-permute-start.3
  380.8 18.3 %collective-permute-start.4 = (f32[2,128,2,1,384]{4,2,1,0,3:T(2,128)S(1)}, f32[2,128,2,1,384]{4,2,1,0,3:T(2,128)S(1)}, u32[]{:S(2)}, u32[]{:S(2)}) collective-permute-start(f32[2,128,2,1,384]{4,2,1,0,3:T(2,128)S(1)} %multiply_add_fusion.4), channel_id=1, source_target_pairs={{0,1},{1,2},{2,3},{3,4},{4,5},{5,6},{6,7},{7,8},{8,9},{9,10},{10,1... | collective-permute-start | bytes 2359304 | tf_op jit(solution)/shard_map/ppermute | solution.py:18
  397.2 4.2 collective-permute-start.5
  408.2 19.5 %collective-permute-start.6 = (f32[2,128,2,1,384]{4,2,1,0,3:T(2,128)S(1)}, f32[2,128,2,1,384]{4,2,1,0,3:T(2,128)}, u32[]{:S(2)}, u32[]{:S(2)}) collective-permute-start(f32[2,128,2,1,384]{4,2,1,0,3:T(2,128)S(1)} %multiply_add_fusion.3), channel_id=1, source_target_pairs={{0,1},{1,2},{2,3},{3,4},{4,5},{5,6},{6,7},{7,8},{8,9},{9,10},{10,1... | collective-permute-start | bytes 2359304 | tf_op jit(solution)/shard_map/ppermute | solution.py:18
  426.0 4.3 collective-permute-start.7
  441.8 67.0 %copy-start.2 = (f32[2,8,256]{2,1,0:T(8,128)S(1)}, f32[2,8,256]{2,1,0:T(8,128)}, u32[]{:S(2)}) copy-start(f32[2,8,256]{2,1,0:T(8,128)} %param.6) | copy-start | bytes 49156
  441.8 67.0 %copy-start.3 = (f32[2,8,256]{2,1,0:T(8,128)S(1)}, f32[2,8,256]{2,1,0:T(8,128)}, u32[]{:S(2)}) copy-start(f32[2,8,256]{2,1,0:T(8,128)} %param.7) | copy-start | bytes 49156
  441.9 66.9 %copy-start.4 = (f32[8]{0:T(128)S(1)}, f32[8]{0:T(128)}, u32[]{:S(2)}) copy-start(f32[8]{0:T(128)} %param.9) | copy-start | bytes 100
  509.1 486.9 %copy-start.1 = (f32[2,8,256]{2,1,0:T(8,128)}, f32[2,8,256]{2,1,0:T(8,128)S(1)}, u32[]{:S(2)}) copy-start(f32[2,8,256]{2,1,0:T(8,128)S(1)} %fusion.8) | copy-start | bytes 49156
  827.2 3.4 collective-permute-start.8
  828.6 5.3 collective-permute-start.9
  841.9 19.8 %collective-permute-start.10 = (f32[2,128,2,1,384]{4,2,1,0,3:T(2,128)S(1)}, f32[2,128,2,1,384]{4,2,1,0,3:T(2,128)S(1)}, u32[]{:S(2)}, u32[]{:S(2)}) collective-permute-start(f32[2,128,2,1,384]{4,2,1,0,3:T(2,128)S(1)} %multiply_add_fusion.2), channel_id=1, source_target_pairs={{0,1},{1,2},{2,3},{3,4},{4,5},{5,6},{6,7},{7,8},{8,9},{9,10},{10,1... | collective-permute-start | bytes 2359304 | tf_op jit(solution)/shard_map/ppermute | solution.py:18
  859.9 4.2 collective-permute-start.11
  870.9 18.3 %collective-permute-start.12 = (f32[2,128,2,1,384]{4,2,1,0,3:T(2,128)S(1)}, f32[2,128,2,1,384]{4,2,1,0,3:T(2,128)S(1)}, u32[]{:S(2)}, u32[]{:S(2)}) collective-permute-start(f32[2,128,2,1,384]{4,2,1,0,3:T(2,128)S(1)} %multiply_add_fusion.1), channel_id=1, source_target_pairs={{0,1},{1,2},{2,3},{3,4},{4,5},{5,6},{6,7},{7,8},{8,9},{9,10},{10,1... | collective-permute-start | bytes 2359304 | tf_op jit(solution)/shard_map/ppermute | solution.py:18
  887.3 4.2 collective-permute-start.13
  898.3 18.9 %collective-permute-start.14 = (f32[2,128,2,1,384]{4,2,1,0,3:T(2,128)S(1)}, f32[2,128,2,1,384]{4,2,1,0,3:T(2,128)S(1)}, u32[]{:S(2)}, u32[]{:S(2)}) collective-permute-start(f32[2,128,2,1,384]{4,2,1,0,3:T(2,128)S(1)} %multiply_add_fusion), channel_id=1, source_target_pairs={{0,1},{1,2},{2,3},{3,4},{4,5},{5,6},{6,7},{7,8},{8,9},{9,10},{10,1... | collective-permute-start | bytes 2359304 | tf_op jit(solution)/shard_map/ppermute | solution.py:18
  915.3 4.2 collective-permute-start.15
Sparse Core Ops, SparseCore 0:
  13.2 323.8 all-reduce.18
  512.9 314.3 all-reduce.20
where the time goes:
time: 1000 us
  waiting for transfers between devices  663 us (66%)
  blocking collectives  134 us (13%)
  starting transfers between devices  117 us (12%)
  other arithmetic  63.2 us (6%)
  between operations  14.4 us (1%)
  matrix products  11.1 us (1%)
    psum x2, waiting for transfers between devices, hessian(): adjoint = lax.psum(partial_value, 'sen')  638 us
    psum x2, blocking collectives, hessian(): forward = lax.psum(forward, 'par')  134 us
    ppermute x8, starting transfers between devices, padded_2(): lax.ppermute(tail, axis, [(i, (i + 1) % count) for i in range(ends)])  106 us
    add x6, other arithmetic, sweep_once(): field + coefficient * (sides[..., :-2] + sides[..., 2:] + upper + linked...  43.3 us
    ppermute x8, waiting for transfers between devices, padded_2(): lax.ppermute(head, axis, [((i + 1) % count, i) for i in range(ends)])  20.8 us
  transfers between devices with their start and end apart: 18, of which 17 were waited for; matrix products, arithmetic and copies ran while one was open for 0% of the time, Pallas kernels for 0%

commit v1 on v0

--- a/solution.py
+++ b/solution.py
@@ -5,6 +5,12 @@
 from jax.sharding import PartitionSpec as P
 
 SWEEPS = 4
+
+
+def gather_and_add(value, axis):
+    terms = lax.all_gather(value, axis, axis=0, tiled=False)
+    acc = terms.sum(axis=0)
+    return acc
 
 
 def padded_2(cells, sides, width):
@@ -86,7 +92,7 @@
         "frs,fsp->frp", spectrum[1], operator[0], preferred_element_type=jnp.float32
     ) - jnp.einsum("frs,fsp->frp", spectrum[0], operator[1], preferred_element_type=jnp.float32)
     partial_value = jnp.stack([real, imag]).reshape(2, half, rows, grid_rows, width)
-    adjoint = lax.psum(partial_value, "sen")
+    adjoint = gather_and_add(partial_value, "sen")
     smoothed = smooth(adjoint, coefficient, offsets, extend_whole)
     prior = smoothed.astype(jnp.bfloat16)
     forward = forward_part(operator, prior)

time: 1000 us -> 984 us (0.984)
  the two profiles are of different devices: /device:TPU:32 before, /device:TPU:8 now
where the time goes in v1:
time: 984 us; the launch traced here: 983 us
  waiting for transfers between devices  621 us (63%)
  blocking collectives  134 us (14%)
  starting transfers between devices  118 us (12%)
  other arithmetic  79.9 us (8%)
  between operations  14.5 us (1%)
  matrix products  11.1 us (1%)
    all_gather x2, waiting for transfers between devices, gather_and_add(): terms = lax.all_gather(value, axis, axis=0, tiled=False)  589 us
    psum x2, blocking collectives, hessian(): forward = lax.psum(forward, 'par')  134 us
    ppermute x8, starting transfers between devices, padded_2(): lax.ppermute(tail, axis, [(i, (i + 1) % count) for i in range(ends)])  107 us
    add x6, other arithmetic, sweep_once(): field + coefficient * (sides[..., :-2] + sides[..., 2:] + upper + linked...  43.6 us
    ppermute x8, waiting for transfers between devices, padded_2(): lax.ppermute(head, axis, [((i + 1) % count, i) for i in range(ends)])  29.1 us
  transfers between devices with their start and end apart: 18, of which 17 were waited for; matrix products, arithmetic and copies ran while one was open for 0% of the time, Pallas kernels for 0%

profile of v1, /device:TPU:8, one launch (start us, length us, event | category | flops | bytes accessed | tf_op | source)
XLA Modules:
  0.0 983.4 jit_solution(6930456843251006270)
XLA Ops:
  8.9 1.6 fusion.64
  13.2 299.9 %all-gather.5.cloned.1.call-done = f32[64,128,2,384]{3,1,2,0:T(8,128)} async-done(((f32[2,128,2,384]{3,1,2,0:T(8,128)}), f32[64,128,2,384]{3,1,2,0:T(8,128)}) %all-gather.5.cloned.1.call-update) | async-done | bytes 25165840 | tf_op jit(solution)/shard_map/all_gather | solution.py:11
  313.1 9.2 reduce.2
  326.1 7.4 collective-permute-done.1
  333.4 9.6 multiply_add_fusion.5
  343.0 18.4 %collective-permute-start.2 = (f32[2,128,2,1,384]{4,2,1,3,0:T(2,128)S(1)}, f32[2,128,2,1,384]{4,2,1,3,0:T(2,128)S(1)}, u32[]{:S(2)}, u32[]{:S(2)}) collective-permute-start(f32[2,128,2,1,384]{4,2,1,3,0:T(2,128)S(1)} %multiply_add_fusion.5), channel_id=1, source_target_pairs={{0,1},{1,2},{2,3},{3,4},{4,5},{5,6},{6,7},{7,8},{8,9},{9,10},{10,1... | collective-permute-start | bytes 2359304 | tf_op jit(solution)/shard_map/ppermute | solution.py:24
  363.3 2.3 collective-permute-done.3
  365.6 6.8 multiply_add_fusion.4
  372.4 16.8 %collective-permute-start.4 = (f32[2,128,2,1,384]{4,2,1,3,0:T(2,128)S(1)}, f32[2,128,2,1,384]{4,2,1,3,0:T(2,128)S(1)}, u32[]{:S(2)}, u32[]{:S(2)}) collective-permute-start(f32[2,128,2,1,384]{4,2,1,3,0:T(2,128)S(1)} %multiply_add_fusion.4), channel_id=1, source_target_pairs={{0,1},{1,2},{2,3},{3,4},{4,5},{5,6},{6,7},{7,8},{8,9},{9,10},{10,1... | collective-permute-start | bytes 2359304 | tf_op jit(solution)/shard_map/ppermute | solution.py:24
  389.2 1.5 collective-permute-start.5
  391.0 2.3 collective-permute-done.5
  393.4 6.8 multiply_add_fusion.3
  400.2 17.5 %collective-permute-start.6 = (f32[2,128,2,1,384]{4,2,1,3,0:T(2,128)S(1)}, f32[2,128,2,1,384]{4,2,1,3,0:T(2,128)}, u32[]{:S(2)}, u32[]{:S(2)}) collective-permute-start(f32[2,128,2,1,384]{4,2,1,3,0:T(2,128)S(1)} %multiply_add_fusion.3), channel_id=1, source_target_pairs={{0,1},{1,2},{2,3},{3,4},{4,5},{5,6},{6,7},{7,8},{8,9},{9,10},{10,1... | collective-permute-start | bytes 2359304 | tf_op jit(solution)/shard_map/ppermute | solution.py:24
  419.1 2.8 collective-permute-done.7
  421.9 9.9 %add_convert_fusion.1 = bf16[2,128,2,1,384]{4,2,1,3,0:T(2,128)(2,1)S(1)} fusion(f32[2,128,2,1,384]{4,2,1,3,0:T(2,128)S(1)} %multiply_add_fusion.3, f32[2,128,2,1,384]{4,2,1,3,0:T(2,128)} %collective-permute-done.6, f32[2,128,2,1,384]{4,2,1,3,0:T(2,128)} %collective-permute-done.7, pred[384]{0:T(512)(128)(4,1)S(1)} %get-tuple-element.7, ...), kind=kLoop, calls=%fused_computation.122 | loop fusion | flops 4128768 | bytes 2756736 | tf_op jit(solution)/shard_map/convert_element_type | solution.py:97
  434.1 66.6 %psum.14 = f32[2,8,256]{2,1,0:T(8,128)S(1)} all-reduce(f32[2,8,256]{2,1,0:T(8,128)S(1)} %copy_bitcast_fusion.3), channel_id=1, replica_groups=mesh['sen'=32,'par'=16] {'par'}, use_global_device_ids=true, to_apply=%region_1.2 | all-reduce | flops 4096 | bytes 32768 | tf_op jit(solution)/shard_map/psum | solution.py:99
  504.7 289.1 %all-gather.7.cloned.1.call-done = f32[64,128,2,384]{3,1,2,0:T(8,128)} async-done(((f32[2,128,2,384]{3,1,2,0:T(8,128)}), f32[64,128,2,384]{3,1,2,0:T(8,128)}) %all-gather.7.cloned.1.call-update) | async-done | bytes 25165840 | tf_op jit(solution)/shard_map/all_gather | solution.py:11
  793.7 9.2 reduce.3
  803.5 1.3 collective-permute-start.8
  804.8 1.5 collective-permute-start.9
  806.7 7.2 collective-permute-done.9
  813.9 6.8 multiply_add_fusion.2
  820.7 18.4 %collective-permute-start.10 = (f32[2,128,2,1,384]{4,2,1,3,0:T(2,128)S(1)}, f32[2,128,2,1,384]{4,2,1,3,0:T(2,128)S(1)}, u32[]{:S(2)}, u32[]{:S(2)}) collective-permute-start(f32[2,128,2,1,384]{4,2,1,3,0:T(2,128)S(1)} %multiply_add_fusion.2), channel_id=1, source_target_pairs={{0,1},{1,2},{2,3},{3,4},{4,5},{5,6},{6,7},{7,8},{8,9},{9,10},{10,1... | collective-permute-start | bytes 2359304 | tf_op jit(solution)/shard_map/ppermute | solution.py:24
  841.0 2.3 collective-permute-done.11
  843.4 6.8 multiply_add_fusion.1
  850.2 16.9 %collective-permute-start.12 = (f32[2,128,2,1,384]{4,2,1,3,0:T(2,128)S(1)}, f32[2,128,2,1,384]{4,2,1,3,0:T(2,128)S(1)}, u32[]{:S(2)}, u32[]{:S(2)}) collective-permute-start(f32[2,128,2,1,384]{4,2,1,3,0:T(2,128)S(1)} %multiply_add_fusion.1), channel_id=1, source_target_pairs={{0,1},{1,2},{2,3},{3,4},{4,5},{5,6},{6,7},{7,8},{8,9},{9,10},{10,1... | collective-permute-start | bytes 2359304 | tf_op jit(solution)/shard_map/ppermute | solution.py:24
  868.9 2.3 collective-permute-done.13
  871.2 6.8 multiply_add_fusion
  878.0 16.5 %collective-permute-start.14 = (f32[2,128,2,1,384]{4,2,1,3,0:T(2,128)S(1)}, f32[2,128,2,1,384]{4,2,1,3,0:T(2,128)S(1)}, u32[]{:S(2)}, u32[]{:S(2)}) collective-permute-start(f32[2,128,2,1,384]{4,2,1,3,0:T(2,128)S(1)} %multiply_add_fusion), channel_id=1, source_target_pairs={{0,1},{1,2},{2,3},{3,4},{4,5},{5,6},{6,7},{7,8},{8,9},{9,10},{10,1... | collective-permute-start | bytes 2359304 | tf_op jit(solution)/shard_map/ppermute | solution.py:24
  896.4 2.3 collective-permute-done.15
  898.8 6.8 add_convert_fusion
  907.8 67.8 %psum.15 = f32[2,8,256]{2,1,0:T(8,128)S(1)} all-reduce(f32[2,8,256]{2,1,0:T(8,128)S(1)} %copy_bitcast_fusion.2), channel_id=1, replica_groups=mesh['sen'=32,'par'=16] {'par'}, use_global_device_ids=true, to_apply=%region_3.4 | all-reduce | flops 4096 | bytes 32768 | tf_op jit(solution)/shard_map/psum | solution.py:99
  (74 shorter events, 27.5 us)
Async XLA Ops:
  7.2 3.3 copy-start
  7.2 305.9 %all-gather.5.cloned.1.call-start = ((), (), s32[]{:S(2)}) async-start(), calls=%async_computation | async-start | bytes 25952256 | tf_op jit(solution)/shard_map/all_gather | solution.py:11
  13.1 780.6 %all-gather.7.cloned.1.call-start = ((), (), s32[]{:S(2)}) async-start(), calls=%async_computation.1 | async-start | bytes 25952256 | tf_op jit(solution)/shard_map/all_gather | solution.py:11
  322.2 3.3 copy-start.5
  322.2 3.3 copy-start.6
  322.9 3.2 collective-permute-start
  324.2 9.2 collective-permute-start.1
  343.0 20.3 %collective-permute-start.2 = (f32[2,128,2,1,384]{4,2,1,3,0:T(2,128)S(1)}, f32[2,128,2,1,384]{4,2,1,3,0:T(2,128)S(1)}, u32[]{:S(2)}, u32[]{:S(2)}) collective-permute-start(f32[2,128,2,1,384]{4,2,1,3,0:T(2,128)S(1)} %multiply_add_fusion.5), channel_id=1, source_target_pairs={{0,1},{1,2},{2,3},{3,4},{4,5},{5,6},{6,7},{7,8},{8,9},{9,10},{10,1... | collective-permute-start | bytes 2359304 | tf_op jit(solution)/shard_map/ppermute | solution.py:24
  361.4 4.2 collective-permute-start.3
  372.4 18.6 %collective-permute-start.4 = (f32[2,128,2,1,384]{4,2,1,3,0:T(2,128)S(1)}, f32[2,128,2,1,384]{4,2,1,3,0:T(2,128)S(1)}, u32[]{:S(2)}, u32[]{:S(2)}) collective-permute-start(f32[2,128,2,1,384]{4,2,1,3,0:T(2,128)S(1)} %multiply_add_fusion.4), channel_id=1, source_target_pairs={{0,1},{1,2},{2,3},{3,4},{4,5},{5,6},{6,7},{7,8},{8,9},{9,10},{10,1... | collective-permute-start | bytes 2359304 | tf_op jit(solution)/shard_map/ppermute | solution.py:24
  389.2 4.2 collective-permute-start.5
  400.2 18.9 %collective-permute-start.6 = (f32[2,128,2,1,384]{4,2,1,3,0:T(2,128)S(1)}, f32[2,128,2,1,384]{4,2,1,3,0:T(2,128)}, u32[]{:S(2)}, u32[]{:S(2)}) collective-permute-start(f32[2,128,2,1,384]{4,2,1,3,0:T(2,128)S(1)} %multiply_add_fusion.3), channel_id=1, source_target_pairs={{0,1},{1,2},{2,3},{3,4},{4,5},{5,6},{6,7},{7,8},{8,9},{9,10},{10,1... | collective-permute-start | bytes 2359304 | tf_op jit(solution)/shard_map/ppermute | solution.py:24
  417.6 4.3 collective-permute-start.7
  433.5 67.2 %copy-start.2 = (f32[2,8,256]{2,1,0:T(8,128)S(1)}, f32[2,8,256]{2,1,0:T(8,128)}, u32[]{:S(2)}) copy-start(f32[2,8,256]{2,1,0:T(8,128)} %param.6) | copy-start | bytes 49156
  433.5 67.2 %copy-start.3 = (f32[2,8,256]{2,1,0:T(8,128)S(1)}, f32[2,8,256]{2,1,0:T(8,128)}, u32[]{:S(2)}) copy-start(f32[2,8,256]{2,1,0:T(8,128)} %param.7) | copy-start | bytes 49156
  433.5 67.2 %copy-start.4 = (f32[8]{0:T(128)S(1)}, f32[8]{0:T(128)}, u32[]{:S(2)}) copy-start(f32[8]{0:T(128)} %param.9) | copy-start | bytes 100
  501.0 474.6 %copy-start.1 = (f32[2,8,256]{2,1,0:T(8,128)}, f32[2,8,256]{2,1,0:T(8,128)S(1)}, u32[]{:S(2)}) copy-start(f32[2,8,256]{2,1,0:T(8,128)S(1)} %fusion.8) | copy-start | bytes 49156
  803.5 3.2 collective-permute-start.8
  804.8 9.1 collective-permute-start.9
  820.7 20.3 %collective-permute-start.10 = (f32[2,128,2,1,384]{4,2,1,3,0:T(2,128)S(1)}, f32[2,128,2,1,384]{4,2,1,3,0:T(2,128)S(1)}, u32[]{:S(2)}, u32[]{:S(2)}) collective-permute-start(f32[2,128,2,1,384]{4,2,1,3,0:T(2,128)S(1)} %multiply_add_fusion.2), channel_id=1, source_target_pairs={{0,1},{1,2},{2,3},{3,4},{4,5},{5,6},{6,7},{7,8},{8,9},{9,10},{10,1... | collective-permute-start | bytes 2359304 | tf_op jit(solution)/shard_map/ppermute | solution.py:24
  839.2 4.2 collective-permute-start.11
  850.2 18.7 %collective-permute-start.12 = (f32[2,128,2,1,384]{4,2,1,3,0:T(2,128)S(1)}, f32[2,128,2,1,384]{4,2,1,3,0:T(2,128)S(1)}, u32[]{:S(2)}, u32[]{:S(2)}) collective-permute-start(f32[2,128,2,1,384]{4,2,1,3,0:T(2,128)S(1)} %multiply_add_fusion.1), channel_id=1, source_target_pairs={{0,1},{1,2},{2,3},{3,4},{4,5},{5,6},{6,7},{7,8},{8,9},{9,10},{10,1... | collective-permute-start | bytes 2359304 | tf_op jit(solution)/shard_map/ppermute | solution.py:24
  867.1 4.2 collective-permute-start.13
  878.0 18.4 %collective-permute-start.14 = (f32[2,128,2,1,384]{4,2,1,3,0:T(2,128)S(1)}, f32[2,128,2,1,384]{4,2,1,3,0:T(2,128)S(1)}, u32[]{:S(2)}, u32[]{:S(2)}) collective-permute-start(f32[2,128,2,1,384]{4,2,1,3,0:T(2,128)S(1)} %multiply_add_fusion), channel_id=1, source_target_pairs={{0,1},{1,2},{2,3},{3,4},{4,5},{5,6},{6,7},{7,8},{8,9},{9,10},{10,1... | collective-permute-start | bytes 2359304 | tf_op jit(solution)/shard_map/ppermute | solution.py:24
  894.6 4.2 collective-permute-start.15
Sparse Core Ops, SparseCore 0:
  13.2 299.7 all-gather.4
  504.8 288.8 all-gather.6
